TPU v7x, 32 devices: a whole 2x2x4 slice. The times are simulated.
32 devices in a mesh: section: 4 (over y, x), ctx: 4 (over z), tp: 2 (over core).
Axes of the slice: x: 2, y: 2, z: 4, core: 2. Of those that a mesh axis runs over, the one named last changes fastest.
Arguments:
- queries: bfloat16 [2048, 8, 8, 128], P('ctx', 'tp', 'section'), may hold values from -44 to 44
- key_states: bfloat16 [2048, 8, 128], P('ctx', 'tp'), may hold values from -4 to 4
- value_states: bfloat16 [2048, 8, 128], P('ctx', 'tp'), may hold values from -6 to 6
- out_grad: bfloat16 [2048, 8, 8, 128], P('ctx', 'tp', 'section'), may hold values from -6 to 6
- band_offsets: int32 [16, 3], replicated, may hold values from -1 to 4, as said below
- global_blocks: int32 [16, 4], replicated, may hold values from -1 to 8, as said below
Outputs:
- attended: bfloat16 [2048, 8, 8, 128], P('ctx', 'tp', 'section')
- query_grad: float32 [2048, 8, 8, 128], P('ctx', 'tp', 'section')
- key_grad: float32 [2048, 8, 128], P('ctx', 'tp')
- value_grad: float32 [2048, 8, 128], P('ctx', 'tp')
Inputs may be any that keep to these rules, and one draw needn't show every extreme that they name: `band_offsets`: in every row r the first offset is 0, the second lies in 1 to 2 and the third in 3 to 4; an offset larger than r is replaced by -1. `global_blocks`: entry n of row r is either -1 or n * 4, and it is n * 4 only when n * 4 < r - 4.
All inputs are finite; a program needn't handle non-finite values.
Results may differ from a plain program's by a relative error of at most 0.017.
Values may be sent and summed in bfloat16 or wider, within the bound.
A program may use at most 128 MiB of HBM per device.

v0:
```python
import jax
import jax.numpy as jnp
from jax import lax
from jax.sharding import PartitionSpec as P

BLK = 128
NBAND = 3
NGLOB = 4


def passed_along(shard, axis, by):
    count = lax.axis_size(axis)
    pairs = [(i, i + by) for i in range(count) if 0 <= i + by < count]
    return lax.ppermute(shard, axis, pairs)


def shards(queries, key_states, value_states, out_grad, band_offsets, global_blocks):
    tok_rows, kv_local, group_local, head_dim = queries.shape
    own_blocks = tok_rows // BLK
    ctx_count = lax.axis_size("ctx")
    all_blocks = own_blocks * ctx_count
    stride_blocks = all_blocks // NGLOB
    stride_devices = stride_blocks // own_blocks
    position = lax.axis_index("ctx")
    scale_factor = head_dim ** (-0.5)
    paired = jnp.stack([key_states, value_states])
    earlier = passed_along(paired, "ctx", 1)
    leading = paired[:, :BLK]
    every_first = lax.all_gather(leading, "ctx", axis=1, tiled=True)
    grouped = every_first.reshape(2, ctx_count, BLK, kv_local, head_dim)[:, ::stride_devices]
    global_rows = grouped.reshape(2, NGLOB * BLK, kv_local, head_dim)
    buffer_blocks = 2 * own_blocks + NGLOB
    stacked = jnp.concatenate([earlier, paired, global_rows], axis=1).reshape(
        2, buffer_blocks, BLK, kv_local, head_dim
    )
    offsets = lax.dynamic_slice_in_dim(band_offsets, position * own_blocks, own_blocks, 0)
    chosen_globals = lax.dynamic_slice_in_dim(global_blocks, position * own_blocks, own_blocks, 0)
    local_rows = jnp.arange(own_blocks, dtype=jnp.int32)[:, None]
    band_ids = own_blocks + local_rows - offsets
    glob_ids = 2 * own_blocks + chosen_globals // stride_blocks
    usable = jnp.concatenate([offsets >= 0, chosen_globals >= 0], axis=1)
    block_ids = jnp.where(usable, jnp.concatenate([band_ids, glob_ids], axis=1), 0)
    key_sel = stacked[0][block_ids]
    value_sel = stacked[1][block_ids]
    query_rows = queries.reshape(own_blocks, BLK, kv_local, group_local, head_dim)
    grad_rows = out_grad.reshape(own_blocks, BLK, kv_local, group_local, head_dim)
    scores = (
        jnp.einsum("rihgd,rnjhd->rhginj", query_rows, key_sel, preferred_element_type=jnp.float32)
        * scale_factor
    )
    lower_half = jnp.arange(BLK)[:, None] >= jnp.arange(BLK)[None, :]
    first_slot = jnp.arange(NBAND + NGLOB) == 0
    reach = jnp.logical_not(first_slot)[None, :, None] | lower_half[:, None, :]
    allowed = usable[:, None, None, None, :, None] & reach[None, None, None]
    scores = jnp.where(allowed, scores, -jnp.inf)
    row_top = jnp.max(scores, axis=(4, 5), keepdims=True)
    probs = jnp.exp(scores - row_top)
    row_total = jnp.sum(probs, axis=(4, 5), keepdims=True)
    weights = probs / row_total
    weights_low = weights.astype(jnp.bfloat16)
    attended = jnp.einsum(
        "rhginj,rnjhd->rihgd", weights_low, value_sel, preferred_element_type=jnp.float32
    ).astype(jnp.bfloat16)
    row_dots = jnp.sum(grad_rows.astype(jnp.float32) * attended.astype(jnp.float32), axis=-1)
    row_dots = jnp.transpose(row_dots, (0, 2, 3, 1))
    dweights = jnp.einsum(
        "rihgd,rnjhd->rhginj", grad_rows, value_sel, preferred_element_type=jnp.float32
    )
    dscores = (weights * (dweights - row_dots[..., None, None])).astype(jnp.bfloat16)
    query_grad = scale_factor * jnp.einsum(
        "rhginj,rnjhd->rihgd", dscores, key_sel, preferred_element_type=jnp.float32
    )
    key_part = scale_factor * jnp.einsum(
        "rhginj,rihgd->rnjhd", dscores, query_rows, preferred_element_type=jnp.float32
    )
    value_part = jnp.einsum(
        "rhginj,rihgd->rnjhd", weights_low, grad_rows, preferred_element_type=jnp.float32
    )
    slot_count = own_blocks * (NBAND + NGLOB)
    target_ids = jnp.where(usable, block_ids, buffer_blocks).reshape(slot_count)

    def place_blocks(part_grad):
        flat_grad = part_grad.reshape(slot_count, BLK, kv_local, head_dim)
        placed = jax.ops.segment_sum(flat_grad, target_ids, num_segments=buffer_blocks + 1)
        return placed[:buffer_blocks]

    block_grads = jnp.stack([place_blocks(key_part), place_blocks(value_part)])
    earlier_grads = block_grads[:, :own_blocks].reshape(2, tok_rows, kv_local, head_dim)
    own_grads = block_grads[:, own_blocks : 2 * own_blocks].reshape(2, tok_rows, kv_local, head_dim)
    global_grads = block_grads[:, 2 * own_blocks :]
    returned = passed_along(earlier_grads.astype(jnp.bfloat16), "ctx", -1).astype(
        earlier_grads.dtype
    )
    own_grads = own_grads + returned
    owner_mask = (jnp.arange(NGLOB) * stride_devices == position).astype(jnp.float32)
    summed = lax.psum(global_grads.astype(jnp.bfloat16), "ctx").astype(jnp.float32)
    owner_rows = jnp.einsum("g,cgjhd->cjhd", owner_mask, summed, precision=lax.Precision.HIGHEST)
    totals = lax.psum(
        jnp.concatenate([own_grads[:, :BLK] + owner_rows, own_grads[:, BLK:]], axis=1), "section"
    )
    return (
        attended.reshape(tok_rows, kv_local, group_local, head_dim),
        query_grad.reshape(tok_rows, kv_local, group_local, head_dim),
        totals[0],
        totals[1],
    )


def solution(mesh):
    placed = (
        P("ctx", "tp", "section", None),
        P("ctx", "tp", None),
        P("ctx", "tp", None),
        P("ctx", "tp", "section", None),
        P(),
        P(),
    )
    return jax.shard_map(
        shards,
        mesh=mesh,
        in_specs=placed,
        out_specs=(
            P("ctx", "tp", "section", None),
            P("ctx", "tp", "section", None),
            P("ctx", "tp", None),
            P("ctx", "tp", None),
        ),
        check_vma=False,
    )
```

profile of v0, /device:TPU:0, one launch (start us, length us, event | category | flops | bytes accessed | tf_op | source)
XLA Modules:
  0.0 332.9 jit_solution(10869660269288517391)
XLA Ops:
  10.6 6.0 %collective-permute-start = (bf16[2,512,4,128]{3,1,2,0:T(8,128)(2,1)}, bf16[2,512,4,128]{3,1,2,0:T(8,128)(2,1)}, u32[]{:S(2)}, u32[]{:S(2)}) collective-permute-start(bf16[2,512,4,128]{3,1,2,0:T(8,128)(2,1)} %pad_maximum_fusion.3), channel_id=1, source_target_pairs={{0,2},{2,4},{4,6},{1,3},{3,5},{5,7},{8,10},{10,12},{12,14},{9,11},... | collective-permute-start | bytes 3145736 | tf_op jit(solution)/shard_map/ppermute | solution.py:14
  19.4 35.7 %collective-permute-done = bf16[2,512,4,128]{3,1,2,0:T(8,128)(2,1)} collective-permute-done((bf16[2,512,4,128]{3,1,2,0:T(8,128)(2,1)}, bf16[2,512,4,128]{3,1,2,0:T(8,128)(2,1)}, u32[]{:S(2)}, u32[]{:S(2)}) %collective-permute-start) | collective-permute-done | bytes 1048608 | tf_op jit(solution)/shard_map/ppermute | solution.py:14
  58.2 2.9 gather_fusion.1
  61.1 8.5 %fusion.4 = (f32[4,4,2,128]{3,2,1,0:T(2,128)S(1)}, f32[4,4,7,128,128,2]{4,3,5,2,1,0:T(8,128)}) fusion(pred[4,128,7,128]{1,3,2,0:T(8,128)(4,1)S(1)} %broadcast_and_fusion, bf16[4,128,4,2,128,1]{4,3,2,1,0,5:T(2,128)(2,1)S(1)} %bitcast.99, bf16[4,7,128,4,128,1]{4,2,3,1,0,5:T(8,128)(2,1)} %bitcast.110), kind=kOutput, calls=%fused_computation.11 | convolution fusion | flops 950530048 | bytes 19873792 | tf_op jit(solution)/shard_map/rihgd,rnjhd->rhginj/dot_general | solution.py:48
  69.5 8.2 %fusion.3 = f32[4,4,2,128]{3,2,1,0:T(2,128)S(1)} fusion(f32[4,4,7,128,128,2]{4,3,5,2,1,0:T(8,128)} %get-tuple-element.23, f32[4,4,2,128]{3,2,1,0:T(2,128)S(1)} %get-tuple-element.22, pred[4,128,7,128]{1,3,2,0:T(8,128)(4,1)S(1)} %broadcast_and_fusion), kind=kLoop, calls=%fused_computation.10 | loop fusion | flops 14675968 | bytes 15171584 | tf_op jit(solution)/shard_map/reduce_sum | solution.py:58
  77.8 9.6 %fusion.16 = bf16[4,4,2,128,7,128]{3,5,2,4,1,0:T(8,128)(2,1)} fusion(f32[4,4,2,128]{3,2,1,0:T(2,128)S(1)} %fusion.3, f32[4,4,2,128]{3,2,1,0:T(2,128)S(1)} %get-tuple-element.22, f32[4,4,7,128,128,2]{4,3,5,2,1,0:T(8,128)} %get-tuple-element.23, pred[4,128,7,128]{1,3,2,0:T(8,128)(4,1)S(1)} %broadcast_and_fusion), kind=kLoop, calls=%fused_computation.31 | loop fusion | flops 18350080 | bytes 22511616 | tf_op jit(solution)/shard_map/convert_element_type | solution.py:60
  87.5 2.9 gather_fusion
  90.4 8.5 %convolution_bitcast_fusion = f32[4,7,128,4,128]{4,2,1,3,0:T(8,128)} fusion(bf16[4,4,2,128,7,128]{3,5,2,4,1,0:T(8,128)(2,1)} %fusion.16, bf16[4,128,4,2,128,1]{4,1,0,3,2,5:T(8,128)(2,1)} %bitcast.107), kind=kOutput, calls=%fused_computation.30 | convolution fusion | flops 939524096 | bytes 15728640 | tf_op jit(solution)/shard_map/rhginj,rihgd->rnjhd/dot_general | solution.py:76
  98.8 6.6 %multiply_reduce_fusion = (f32[4,128,4,2]{1,3,2,0:T(2,128)S(1)}, bf16[4,128,4,2,128]{4,1,3,2,0:T(8,128)(2,1)}) fusion(bf16[4,128,4,2,128]{4,1,0,3,2:T(8,128)(2,1)S(1)} %bitcast.108, bf16[4,4,2,128,7,128]{3,5,2,4,1,0:T(8,128)(2,1)} %fusion.16, bf16[4,7,128,4,128,1]{4,2,3,1,0,5:T(8,128)(2,1)S(1)} %bitcast.112), kind=kOutput, calls=%fused_computation.38 | convolution fusion | flops 942141440 | bytes 13123584 | tf_op jit(solution)/shard_map/rhginj,rnjhd->rihgd/dot_general | solution.py:61
  105.5 8.0 %fusion.1 = bf16[4,4,2,128,7,128]{3,5,2,4,1,0:T(8,128)(2,1)S(1)} fusion(f32[4,4,2,128]{3,2,1,0:T(2,128)S(1)} %bitcast.119, bf16[4,7,128,4,128,1]{4,2,3,1,0,5:T(8,128)(2,1)S(1)} %bitcast.113, f32[4,4,2,128]{3,2,1,0:T(2,128)S(1)} %fusion.3, f32[4,4,2,128]{3,2,1,0:T(2,128)S(1)} %get-tuple-element.22, f32[4,4,7,128,128,2]{4,3,5,2,1,0:T(8,128)} %get-tuple-element.23, ...), kind=kOutput, calls=%fused_computation.6 | convolution fusion | flops 965214208 | bytes 27246592 | tf_op jit(solution)/shard_map/rihgd,rnjhd->rhginj/dot_general | solution.py:66
  116.4 4.0 %copy.103 = f32[4,7,128,4,128]{4,2,3,1,0:T(8,128)} copy(f32[4,7,128,4,128]{4,2,1,3,0:T(8,128)S(1)} %fusion.5) | data formatting | bytes 14680064 | tf_op jit(solution)/shard_map/mul | solution.py:73
  120.4 2.2 broadcast.117.clone
  122.6 17.9 %scatter_fusion = f32[13,128,4,128]{3,1,2,0:T(8,128)} fusion(f32[13,128,4,128]{3,1,2,0:T(8,128)} %broadcast.117.clone, s32[28]{0:T(128)S(1)} %fusion.42, f32[28,128,4,128]{3,1,2,0:T(8,128)} %bitcast.102), kind=kCustom, calls=%fused_computation.2 | custom fusion | flops 1835008 | bytes 22020208 | tf_op jit(solution)/shard_map/scatter-add | solution.py:84
  140.5 3.9 %slice_bitcast_fusion.1 = f32[1,12,128,4,128]{4,2,3,1,0:T(8,128)} fusion(f32[13,128,4,128]{3,1,2,0:T(8,128)} %scatter_fusion), kind=kLoop, calls=%fused_computation.28 | loop fusion | bytes 6291456 | tf_op jit(solution)/shard_map/stack | solution.py:87
  144.4 7.0 %copy.105 = f32[4,7,128,4,128]{4,2,3,1,0:T(8,128)} copy(f32[4,7,128,4,128]{4,2,1,3,0:T(8,128)} %convolution_bitcast_fusion) | data formatting | bytes 14680064 | tf_op jit(solution)/shard_map/rhginj,rihgd->rnjhd/transpose | solution.py:76
  151.5 2.1 broadcast.117.clone.1
  153.6 17.1 %scatter_fusion.1 = f32[13,128,4,128]{3,1,2,0:T(8,128)} fusion(f32[13,128,4,128]{3,1,2,0:T(8,128)} %broadcast.117.clone.1, s32[28]{0:T(128)S(1)} %fusion.42, f32[28,128,4,128]{3,1,2,0:T(8,128)} %bitcast.101), kind=kCustom, calls=%fused_computation.3 | custom fusion | flops 1835008 | bytes 22020208 | tf_op jit(solution)/shard_map/scatter-add | solution.py:84
  170.8 2.2 slice_bitcast_fusion
  180.0 40.9 %collective-permute-done.1 = bf16[2,512,4,128]{3,1,2,0:T(8,128)(2,1)S(1)} collective-permute-done((bf16[2,512,4,128]{3,1,2,0:T(8,128)(2,1)S(1)}, bf16[2,512,4,128]{3,1,2,0:T(8,128)(2,1)S(1)}, u32[]{:S(2)}, u32[]{:S(2)}) %collective-permute-start.1) | collective-permute-done | bytes 1048608 | tf_op jit(solution)/shard_map/ppermute | solution.py:14
  222.4 26.3 %all-reduce.3.cloned.1.call-done = bf16[2,4,128,4,128]{4,2,3,1,0:T(8,128)(2,1)} async-done(((bf16[2,4,128,4,128]{4,2,3,1,0:T(8,128)(2,1)}), bf16[2,4,128,4,128]{4,2,3,1,0:T(8,128)(2,1)}) %all-reduce.3.cloned.1.call-update) | async-done | bytes 1048592 | tf_op jit(solution)/shard_map/psum | solution.py:96
  248.7 2.2 fusion.32
  254.7 5.9 %fusion.18 = f32[4,128,4,2,128]{4,1,3,2,0:T(8,128)S(1)} fusion(bf16[4,4,2,128,7,128]{3,5,2,4,1,0:T(8,128)(2,1)} %copy-done.4, bf16[4,7,128,4,128,1]{4,2,3,1,0,5:T(8,128)(2,1)S(1)} %bitcast.111), kind=kOutput, calls=%fused_computation.36 | convolution fusion | flops 940048384 | bytes 13107200 | tf_op jit(solution)/shard_map/rhginj,rnjhd->rihgd/dot_general | solution.py:70
  260.8 2.9 copy.109
  263.8 57.6 %all-reduce.5.cloned.1.call-done = f32[2,512,4,128]{3,1,2,0:T(8,128)} async-done(((f32[2,512,4,128]{3,1,2,0:T(8,128)}), f32[2,512,4,128]{3,1,2,0:T(8,128)}) %all-reduce.5.cloned.1.call-update) | async-done | bytes 2097168 | tf_op jit(solution)/shard_map/psum | solution.py:98
  (83 shorter events, 29.7 us)
Async XLA Ops:
  7.2 53.9 %copy-start = (bf16[512,4,2,128]{3,2,1,0:T(2,128)(2,1)S(1)}, bf16[512,4,2,128]{3,2,1,0:T(2,128)(2,1)}, u32[]{:S(2)}) copy-start(bf16[512,4,2,128]{3,2,1,0:T(2,128)(2,1)} %param.6) | copy-start | bytes 3145732
  7.2 9.4 %copy-start.12 = (s32[16,4]{0,1:T(4,128)S(1)}, s32[16,4]{0,1:T(4,128)}, u32[]{:S(2)}) copy-start(s32[16,4]{0,1:T(4,128)} %param.11) | copy-start | bytes 772
  7.2 9.6 %copy-start.13 = (s32[16,3]{0,1:T(4,128)S(1)}, s32[16,3]{0,1:T(4,128)}, u32[]{:S(2)}) copy-start(s32[16,3]{0,1:T(4,128)} %param.10) | copy-start | bytes 580
  7.2 10.2 %copy-start.10 = (bf16[512,4,2,128]{3,2,1,0:T(2,128)(2,1)S(1)}, bf16[512,4,2,128]{3,2,1,0:T(2,128)(2,1)}, u32[]{:S(2)}) copy-start(bf16[512,4,2,128]{3,2,1,0:T(2,128)(2,1)} %param.9) | copy-start | bytes 3145732
  7.2 47.9 %all-gather.2.cloned.1.call-start = ((), (), s32[]{:S(2)}) async-start(), calls=%async_computation | async-start | bytes 1310720 | tf_op jit(solution)/shard_map/all_gather | solution.py:29
  9.5 239.2 %all-reduce.3.cloned.1.call-start = ((), (), s32[]{:S(2)}) async-start(), calls=%async_computation.1 | async-start | bytes 2097152 | tf_op jit(solution)/shard_map/psum | solution.py:96
  10.6 44.5 %collective-permute-start = (bf16[2,512,4,128]{3,1,2,0:T(8,128)(2,1)}, bf16[2,512,4,128]{3,1,2,0:T(8,128)(2,1)}, u32[]{:S(2)}, u32[]{:S(2)}) collective-permute-start(bf16[2,512,4,128]{3,1,2,0:T(8,128)(2,1)} %pad_maximum_fusion.3), channel_id=1, source_target_pairs={{0,2},{2,4},{4,6},{1,3},{3,5},{5,7},{8,10},{10,12},{12,14},{9,11},... | collective-permute-start | bytes 3145736 | tf_op jit(solution)/shard_map/ppermute | solution.py:14
  77.8 9.6 %copy-start.5 = (bf16[1,1536,4,128]{3,1,2,0:T(8,128)(2,1)S(1)}, bf16[1,1536,4,128]{3,1,2,0:T(8,128)(2,1)}, u32[]{:S(2)}) copy-start(bf16[1,1536,4,128]{3,1,2,0:T(8,128)(2,1)} %get-tuple-element.18) | copy-start | bytes 4718596
  90.4 8.5 %copy-start.7 = (bf16[512,4,2,128]{3,0,2,1:T(8,128)(2,1)S(1)}, bf16[512,4,2,128]{3,0,2,1:T(8,128)(2,1)}, u32[]{:S(2)}) copy-start(bf16[512,4,2,128]{3,0,2,1:T(8,128)(2,1)} %copy.93) | copy-start | bytes 3145732
  90.4 8.5 %copy-start.9 = (bf16[28,128,4,128]{3,1,2,0:T(8,128)(2,1)S(1)}, bf16[28,128,4,128]{3,1,2,0:T(8,128)(2,1)}, u32[]{:S(2)}) copy-start(bf16[28,128,4,128]{3,1,2,0:T(8,128)(2,1)} %gather_fusion) | copy-start | bytes 11010052
  113.5 2.9 copy-start.4
  170.8 2.8 copy-start.2
  173.6 1.7 copy-start.3
  176.5 44.4 %collective-permute-start.1 = (bf16[2,512,4,128]{3,1,2,0:T(8,128)(2,1)S(1)}, bf16[2,512,4,128]{3,1,2,0:T(8,128)(2,1)S(1)}, u32[]{:S(2)}, u32[]{:S(2)}) collective-permute-start(bf16[2,512,4,128]{3,1,2,0:T(8,128)(2,1)S(1)} %bitcast.114), channel_id=1, source_target_pairs={{2,0},{4,2},{6,4},{3,1},{5,3},{7,5},{10,8},{12,10},{14,12},{11,9},... | collective-permute-start | bytes 3145736 | tf_op jit(solution)/shard_map/ppermute | solution.py:14
  177.8 143.6 %all-reduce.5.cloned.1.call-start = ((), (), s32[]{:S(2)}) async-start(), calls=%async_computation.2 | async-start | bytes 4194304 | tf_op jit(solution)/shard_map/psum | solution.py:98
  248.7 2.3 copy-start.6
  251.0 1.6 copy-start.11
  252.5 2.2 copy-start.8
  260.8 65.6 %copy-start.1 = (bf16[512,4,2,128]{3,2,1,0:T(2,128)(2,1)S(1)}, bf16[512,4,2,128]{3,2,1,0:T(2,128)(2,1)}, u32[]{:S(2)}) copy-start(bf16[512,4,2,128]{3,2,1,0:T(2,128)(2,1)} %param.6) | copy-start | bytes 3145732
Sparse Core Ops, SparseCore 0:
  10.2 44.1 all-gather.1
  177.9 70.6 all-reduce.2
  252.6 68.7 all-reduce.4
where the time goes:
time: 334 us; the launch traced here: 333 us
  waiting for transfers between devices  161 us (48%)
  other arithmetic  61.2 us (18%)
  local copies, waits for them, and re-layouts  47.8 us (14%)
  matrix products  41.8 us (13%)
  between operations  14 us (4%)
  starting transfers between devices  7.61 us (2%)
    ppermute x2, waiting for transfers between devices, passed_along(): return lax.ppermute(shard, axis, pairs)  76.6 us
    psum x1, waiting for transfers between devices, shards(): lax.psum(jnp.concatenate([own_grads[:, :BLK] + owner_rows, own_grads[:, B...  57.6 us
    scatter-add x2, other arithmetic, place_blocks(): jax.ops.segment_sum(flat_grad, target_ids, num_segments=buffer_blocks + 1)  35 us
    psum x1, waiting for transfers between devices, shards(): lax.psum(global_grads.astype(jnp.bfloat16), 'ctx').astype(jnp.float32)  26.3 us
    unnamed x33, local copies, waits for them, and re-layouts  12 us
    convert_element_type x1, other arithmetic, shards(): weights_low = weights.astype(jnp.bfloat16)  9.61 us
    dot_general x1, matrix products, shards(): jnp.einsum('rihgd,rnjhd->rhginj', query_rows, key_sel, preferred_element_...  8.46 us
    dot_general x1, matrix products, shards(): jnp.einsum('rhginj,rihgd->rnjhd', weights_low, grad_rows, preferred_eleme...  8.45 us
  transfers between devices with their start and end apart: 5, of which 4 were waited for; matrix products, arithmetic and copies ran while one was open for 6% of the time, Pallas kernels for 0%

commit v1 on v0

v1 whole, which is shorter than its diff:
```python
import functools

import jax
import jax.numpy as jnp
from jax import lax
from jax.experimental import pallas as pl
from jax.experimental.pallas import tpu as pltpu
from jax.sharding import PartitionSpec as P

BLK = 128
NBAND = 3
NGLOB = 4
REACH = ((1, 2), (3, 4))
LOG2E = 1.4426950408889634
LOW = -1e30


def global_count(all_blocks, stride_blocks, own_blocks):
    return len([n for n in range(NGLOB) if n * stride_blocks < all_blocks - 1 - own_blocks])


def dot_nt(a, b):
    return lax.dot_general(a, b, (((1,), (1,)), ((), ())), preferred_element_type=jnp.float32)


def dot_tn(a, b):
    return lax.dot_general(a, b, (((0,), (0,)), ((), ())), preferred_element_type=jnp.float32)


def dot_nn(a, b):
    return lax.dot_general(a, b, (((1,), (0,)), ((), ())), preferred_element_type=jnp.float32)


def head_rows(own_blocks, n_glob, scale, row_base, band_ref, glob_ref, q_of, g_of, key_of, value_of,
              put_att, put_dq, add_key, add_value):
    for i in range(own_blocks):
        row = row_base + i
        offs = [band_ref[row, 1 + m] for m in range(NBAND - 1)]
        chosen = [glob_ref[row, n] for n in range(n_glob)]
        q, g = q_of(i), g_of(i)

        def selected(block_of):
            parts = [block_of(own_blocks + i)]
            for m in range(NBAND - 1):
                near, far = REACH[m]
                parts.append(jnp.where(offs[m] == near, block_of(own_blocks + i - near),
                                       block_of(own_blocks + i - far)))
            for n in range(n_glob):
                parts.append(block_of(2 * own_blocks + n))
            return jnp.concatenate(parts, axis=0)

        keys, values = selected(key_of), selected(value_of)
        scores = dot_nt(keys, q)
        width = scores.shape[1]
        key_pos = lax.broadcasted_iota(jnp.int32, (BLK, width), 0)
        query_pos = lax.broadcasted_iota(jnp.int32, (BLK, width), 1) % BLK
        usable = [o >= 0 for o in offs] + [c >= 0 for c in chosen]
        pieces = [jnp.where(key_pos <= query_pos, scores[:BLK], LOW)]
        for n, ok in enumerate(usable):
            pieces.append(scores[(n + 1) * BLK:(n + 2) * BLK] + jnp.where(ok, 0.0, LOW))
        scores = jnp.concatenate(pieces, axis=0)
        top = jnp.max(scores, axis=0, keepdims=True)
        probs = jnp.exp2((scores - top) * (scale * LOG2E))
        weights = probs * (1.0 / jnp.sum(probs, axis=0, keepdims=True))
        low = weights.astype(jnp.bfloat16)
        att = dot_tn(values, low).astype(jnp.bfloat16).astype(jnp.float32)
        put_att(i, att.T.astype(jnp.bfloat16))
        dots = jnp.sum(g.astype(jnp.float32).T * att, axis=0, keepdims=True)
        ds = (weights * (dot_nt(values, g) - dots)).astype(jnp.bfloat16)
        put_dq(i, (dot_tn(keys, ds) * scale).T)
        dk, dv = dot_nn(ds, q) * scale, dot_nn(low, g)
        for part, add in ((dk, add_key), (dv, add_value)):
            add(own_blocks + i, part[:BLK])
            for m in range(NBAND - 1):
                piece = part[(m + 1) * BLK:(m + 2) * BLK]
                for off in REACH[m]:
                    add(own_blocks + i - off, jnp.where(offs[m] == off, piece, 0.0))
            for n in range(n_glob):
                at = (NBAND + n) * BLK
                add(2 * own_blocks + n, part[at:at + BLK])


def local_kernel(own_blocks, n_glob, scale, band_ref, glob_ref, q_ref, g_ref, kv_ref, att_ref, dq_ref, grads_ref,
                 acc_ref):
    row_base = lax.axis_index("ctx") * own_blocks
    touched = set()

    def add_to(which):
        def add(slot, part):
            if (which, slot) in touched:
                acc_ref[which, slot] += part
            else:
                acc_ref[which, slot] = part
                touched.add((which, slot))
        return add

    def put_att(i, x):
        att_ref[0, i] = x

    def put_dq(i, x):
        dq_ref[0, i] = x

    head_rows(own_blocks, n_glob, scale, row_base, band_ref, glob_ref,
              lambda i: q_ref[0, i], lambda i: g_ref[0, i],
              lambda slot: kv_ref[0, 0, slot], lambda slot: kv_ref[1, 0, slot],
              put_att, put_dq, add_to(0), add_to(1))
    grads_ref[:, 0] = acc_ref[...].astype(grads_ref.dtype)


def passed_along(shard, axis, by):
    count = lax.axis_size(axis)
    pairs = [(i, i + by) for i in range(count) if 0 <= i + by < count]
    return lax.ppermute(shard, axis, pairs)


def rows_first(x, own_blocks):
    tok, heads, group, dim = x.shape
    x = x.reshape(own_blocks, BLK, heads, group, dim)
    return jnp.transpose(x, (2, 0, 3, 1, 4)).reshape(heads, own_blocks, group * BLK, dim)


def rows_back(x, group):
    heads, own_blocks, _, dim = x.shape
    x = x.reshape(heads, own_blocks, group, BLK, dim)
    return jnp.transpose(x, (1, 3, 0, 2, 4)).reshape(own_blocks * BLK, heads, group, dim)


def shards(queries, key_states, value_states, out_grad, band_offsets, global_blocks):
    tok, heads, group, dim = queries.shape
    own_blocks = tok // BLK
    ctx_count = lax.axis_size("ctx")
    all_blocks = own_blocks * ctx_count
    stride_blocks = all_blocks // NGLOB
    stride_devices = stride_blocks // own_blocks
    n_glob = global_count(all_blocks, stride_blocks, own_blocks)
    position = lax.axis_index("ctx")
    scale = dim ** (-0.5)
    q, g = rows_first(queries, own_blocks), rows_first(out_grad, own_blocks)
    own = jnp.stack([key_states, value_states]).transpose(0, 2, 1, 3).reshape(2, heads, own_blocks, BLK, dim)
    earlier = passed_along(own, "ctx", 1)
    firsts = lax.all_gather(own[:, :, 0], "ctx", axis=2)[:, :, ::stride_devices][:, :, :n_glob]
    stacked = jnp.concatenate([earlier, own, firsts], axis=2)
    slots = 2 * own_blocks + n_glob
    smem = pl.BlockSpec(memory_space=pltpu.SMEM)
    row_spec = pl.BlockSpec((1, own_blocks, group * BLK, dim), lambda h: (h, 0, 0, 0))
    slot_spec = pl.BlockSpec((2, 1, slots, BLK, dim), lambda h: (0, h, 0, 0, 0))
    att, dq, grads = pl.pallas_call(
        functools.partial(local_kernel, own_blocks, n_glob, scale),
        grid=(heads,),
        in_specs=[smem, smem, row_spec, row_spec, slot_spec],
        out_specs=[row_spec, row_spec, slot_spec],
        out_shape=[
            jax.ShapeDtypeStruct(q.shape, jnp.bfloat16),
            jax.ShapeDtypeStruct(q.shape, jnp.float32),
            jax.ShapeDtypeStruct((2, heads, slots, BLK, dim), jnp.bfloat16),
        ],
        scratch_shapes=[pltpu.VMEM((2, slots, BLK, dim), jnp.float32)],
        compiler_params=pltpu.CompilerParams(vmem_limit_bytes=56 * 2**20),
    )(band_offsets, global_blocks, q, g, stacked)
    back = passed_along(grads[:, :, :own_blocks], "ctx", -1)
    own_grads = grads[:, :, own_blocks:2 * own_blocks].astype(jnp.float32) + back.astype(jnp.float32)
    summed = lax.psum(grads[:, :, 2 * own_blocks:], "ctx").astype(jnp.float32)
    mine = (jnp.arange(n_glob) * stride_devices == position)[None, None, :, None, None]
    first = jnp.sum(jnp.where(mine, summed, 0.0), axis=2)
    own_grads = jnp.concatenate([own_grads[:, :, :1] + first[:, :, None], own_grads[:, :, 1:]], axis=2)
    totals = lax.psum(own_grads.astype(jnp.bfloat16), "section").astype(jnp.float32)
    totals = totals.reshape(2, heads, tok, dim).transpose(0, 2, 1, 3)
    return rows_back(att, group), rows_back(dq, group), totals[0], totals[1]


def solution(mesh):
    wide, narrow = P("ctx", "tp", "section", None), P("ctx", "tp", None)
    return jax.shard_map(
        shards,
        mesh=mesh,
        in_specs=(wide, narrow, narrow, wide, P(), P()),
        out_specs=(wide, wide, narrow, narrow),
        check_vma=False,
    )
```

time: 334 us -> 212 us (0.63)
  other arithmetic: 61.2 us -> 9.75 us
  matrix products: 41.8 us -> 0 us
  local copies, waits for them, and re-layouts: 47.8 us -> 17.3 us
  Pallas kernels: 0 us -> 22.4 us
  waiting for transfers between devices: 161 us -> 140 us
    ppermute x2, waiting for transfers between devices: 76.6 us -> 0.26 us  [passed_along(): return lax.ppermute(shard, axis, pairs)]
    dot_general x7 -> x0, matrix products: 41.8 us -> none  [the longest x1 8.46 us: shards(): jnp.einsum('rihgd,rnjhd->rhginj', query_rows, key_sel, preferred_element_...]
    scatter-add x2 -> x0, other arithmetic: 35 us -> none  [place_blocks(): jax.ops.segment_sum(flat_grad, target_ids, num_segments=buffer_blocks + 1)]
    all_gather x1, waiting for transfers between devices: 0.01 us -> 34.2 us  [shards(): lax.all_gather(own[:, :, 0], 'ctx', axis=2)[:, :, ::stride_devices]]
    pallas_call x0 -> x1, Pallas kernels: none -> 22.4 us  [shards(): pl.pallas_call(functools.partial(local_kernel, own_blocks, n_glob, scale)...]
    psum x2, waiting for transfers between devices: 83.9 us -> 106 us  [the longest x1 58.8 us: shards(): summed = lax.psum(grads[:, :, 2 * own_blocks:], 'ctx').astype(jnp.float32)]
    another operation x5 -> x0, local copies, waits for them, and re-layouts: 12 us -> none  [the longest x2 6.17 us: shards(): block_grads = jnp.stack([place_blocks(key_part), place_blocks(value_part)])]
    unnamed x33 -> x14, local copies, waits for them, and re-layouts: 12 us -> 1.36 us
where the time goes in v1:
time: 212 us; the launch traced here: 211 us
  waiting for transfers between devices  140 us (66%)
  Pallas kernels  22.4 us (11%)
  local copies, waits for them, and re-layouts  17.3 us (8%)
  between operations  13.9 us (7%)
  other arithmetic  9.75 us (5%)
  starting transfers between devices  7.53 us (4%)
    psum x1, waiting for transfers between devices, shards(): summed = lax.psum(grads[:, :, 2 * own_blocks:], 'ctx').astype(jnp.float32)  58.8 us
    psum x1, waiting for transfers between devices, shards(): lax.psum(own_grads.astype(jnp.bfloat16), 'section').astype(jnp.float32)  46.8 us
    all_gather x1, waiting for transfers between devices, shards(): lax.all_gather(own[:, :, 0], 'ctx', axis=2)[:, :, ::stride_devices]  34.2 us
    pallas_call x1, Pallas kernels, shards(): pl.pallas_call(functools.partial(local_kernel, own_blocks, n_glob, scale)...  22.4 us
    ppermute x2, starting transfers between devices, passed_along(): return lax.ppermute(shard, axis, pairs)  7.23 us
    transpose x2, local copies, waits for them, and re-layouts, rows_back(): jnp.transpose(x, (1, 3, 0, 2, 4))  4.99 us
  transfers between devices with their start and end apart: 5, of which 4 were waited for; matrix products, arithmetic and copies ran while one was open for 6% of the time, Pallas kernels for 0%

profile of v1, /device:TPU:0, one launch (start us, length us, event | category | flops | bytes accessed | tf_op | source)
XLA Modules:
  0.0 211.0 jit_solution(2492562716740893058)
XLA Ops:
  7.2 2.1 maximum_bitcast_fusion
  9.5 0.7 slice.37
  10.2 5.9 %collective-permute-start = (bf16[2,4,4,128,128]{4,3,2,1,0:T(8,128)(2,1)S(1)}, bf16[2,4,4,128,128]{4,3,2,1,0:T(8,128)(2,1)}, u32[]{:S(2)}, u32[]{:S(2)}) collective-permute-start(bf16[2,4,4,128,128]{4,3,2,1,0:T(8,128)(2,1)S(1)} %bitcast.32), channel_id=1, source_target_pairs={{0,2},{2,4},{4,6},{1,3},{3,5},{5,7},{8,10},{10,12},{12,14},{9,11},... | collective-permute-start | bytes 3145736 | tf_op jit(solution)/shard_map/ppermute | solution.py:113
  16.2 1.2 copy.10
  17.4 1.2 copy.11
  18.6 0.7 copy.13.band_ref
  19.3 0.7 copy.14.glob_ref
  20.0 34.2 %all-gather.2.cloned.1.call-done = bf16[2,4,4,128,128]{4,3,2,1,0:T(8,128)(2,1)} async-done(((bf16[2,4,1,128,128]{4,3,2,1,0:T(8,128)(2,1)}), bf16[2,4,4,128,128]{4,3,2,1,0:T(8,128)(2,1)}) %all-gather.2.cloned.1.call-update) | async-done | bytes 1048592 | tf_op jit(solution)/shard_map/all_gather | solution.py:141
  54.2 0.3 collective-permute-done
  54.5 0.9 slice-done
  55.3 3.2 %pad_maximum_fusion.kv_ref = bf16[2,4,11,128,128]{4,3,2,1,0:T(8,128)(2,1)} fusion(bf16[2,4,3,128,128]{4,3,2,1,0:T(8,128)(2,1)S(1)} %slice-done, bf16[2,4,4,128,128]{4,3,2,1,0:T(8,128)(2,1)S(1)} %bitcast.33, bf16[2,4,4,128,128]{4,3,2,1,0:T(8,128)(2,1)} %collective-permute-done), kind=kLoop, calls=%fused_computation | loop fusion | flops 2883584 | bytes 5767168 | tf_op jit(solution)/shard_map/concatenate | solution.py:142
  58.5 22.4 %shard_map.93 = (bf16[4,4,256,128]{3,2,1,0:T(8,128)(2,1)}, f32[4,4,256,128]{3,2,1,0:T(8,128)}, bf16[2,4,11,128,128]{4,3,2,1,0:T(8,128)(2,1)}) custom-call(s32[16,3]{1,0:T(8,128)} %copy.13.band_ref, s32[16,4]{1,0:T(8,128)} %copy.14.glob_ref, bf16[4,4,256,128]{3,2,1,0:T(8,128)(2,1)} %bitcast.34, bf16[4,4,256,128]{3,2,1,0:T(8,128)(2,1)} %bitcast.35, ...), custom_call_target="tpu_custom_call" | custom-call | tf_op jit(solution)/shard_map/pallas_call | solution.py:147
  80.9 1.3 slice.31
  82.2 1.3 collective-permute-start.1
  83.5 2.1 slice.33
  85.8 58.8 %all-reduce.3.cloned.1.call-done = bf16[2,4,3,128,128]{4,3,2,1,0:T(8,128)(2,1)} async-done(((bf16[2,4,3,128,128]{4,3,2,1,0:T(8,128)(2,1)}), bf16[2,4,3,128,128]{4,3,2,1,0:T(8,128)(2,1)}) %all-reduce.3.cloned.1.call-update) | async-done | bytes 786448 | tf_op jit(solution)/shard_map/psum | solution.py:162
  144.6 1.4 select_reduce_fusion
  146.1 1.6 convert_add_fusion
  148.0 1.8 copy.19
  149.8 2.9 %copy.16 = f32[4,128,4,2,128]{4,3,2,1,0:T(2,128)} copy(f32[4,128,4,2,128]{4,1,3,0,2:T(8,128)S(1)} %bitcast.38) | data formatting | bytes 4194304 | tf_op jit(solution)/shard_map/transpose | solution.py:125
  152.8 2.0 copy.15
  154.8 46.8 %all-reduce.5.cloned.1.call-done = bf16[2,512,4,128]{3,2,1,0:T(4,128)(2,1)} async-done(((bf16[2,512,4,128]{3,2,1,0:T(4,128)(2,1)}), bf16[2,512,4,128]{3,2,1,0:T(4,128)(2,1)}) %all-reduce.5.cloned.1.call-update) | async-done | bytes 1048592 | tf_op jit(solution)/shard_map/psum | solution.py:166
  201.7 1.4 transpose.28
  203.0 1.5 slice_bitcast_fusion
  (25 shorter events, 0.8 us)
Async XLA Ops:
  7.2 47.0 %all-gather.2.cloned.1.call-start = ((), (), s32[]{:S(2)}) async-start(), calls=%async_computation | async-start | bytes 1310720 | tf_op jit(solution)/shard_map/all_gather | solution.py:141
  7.2 9.0 %copy-start.1 = (bf16[512,4,2,128]{3,2,1,0:T(2,128)(2,1)S(1)}, bf16[512,4,2,128]{3,2,1,0:T(2,128)(2,1)}, u32[]{:S(2)}) copy-start(bf16[512,4,2,128]{3,2,1,0:T(2,128)(2,1)} %param.6) | copy-start | bytes 3145732
  9.3 8.1 %copy-start.2 = (bf16[512,4,2,128]{3,2,1,0:T(2,128)(2,1)S(1)}, bf16[512,4,2,128]{3,2,1,0:T(2,128)(2,1)}, u32[]{:S(2)}) copy-start(bf16[512,4,2,128]{3,2,1,0:T(2,128)(2,1)} %param.9) | copy-start | bytes 3145732
  10.2 134.4 %all-reduce.3.cloned.1.call-start = ((), (), s32[]{:S(2)}) async-start(), calls=%async_computation.1 | async-start | bytes 1572864 | tf_op jit(solution)/shard_map/psum | solution.py:162
  10.2 44.2 %collective-permute-start = (bf16[2,4,4,128,128]{4,3,2,1,0:T(8,128)(2,1)S(1)}, bf16[2,4,4,128,128]{4,3,2,1,0:T(8,128)(2,1)}, u32[]{:S(2)}, u32[]{:S(2)}) collective-permute-start(bf16[2,4,4,128,128]{4,3,2,1,0:T(8,128)(2,1)S(1)} %bitcast.32), channel_id=1, source_target_pairs={{0,2},{2,4},{4,6},{1,3},{3,5},{5,7},{8,10},{10,12},{12,14},{9,11},... | collective-permute-start | bytes 3145736 | tf_op jit(solution)/shard_map/ppermute | solution.py:113
  16.2 2.4 %copy-start.4 = (s32[16,3]{0,1:T(4,128)S(1)}, s32[16,3]{0,1:T(4,128)}, u32[]{:S(2)}) copy-start(s32[16,3]{0,1:T(4,128)} %param.10) | copy-start | bytes 580
  16.2 3.1 %copy-start.5 = (s32[16,4]{0,1:T(4,128)S(1)}, s32[16,4]{0,1:T(4,128)}, u32[]{:S(2)}) copy-start(s32[16,4]{0,1:T(4,128)} %param.11) | copy-start | bytes 772
  54.2 1.1 slice-start
  82.2 63.9 %collective-permute-start.1 = (bf16[2,4,4,128,128]{4,3,2,1,0:T(8,128)(2,1)S(1)}, bf16[2,4,4,128,128]{4,3,2,1,0:T(8,128)(2,1)S(1)}, u32[]{:S(2)}, u32[]{:S(2)}) collective-permute-start(bf16[2,4,4,128,128]{4,3,2,1,0:T(8,128)(2,1)S(1)} %slice.31), channel_id=1, source_target_pairs={{2,0},{4,2},{6,4},{3,1},{5,3},{7,5},{10,8},{12,10},{14,12},{11,9},... | collective-permute-start | bytes 3145736 | tf_op jit(solution)/shard_map/ppermute | solution.py:113
  85.6 116.1 %all-reduce.5.cloned.1.call-start = ((), (), s32[]{:S(2)}) async-start(), calls=%async_computation.2 | async-start | bytes 2097152 | tf_op jit(solution)/shard_map/psum | solution.py:166
  148.0 1.8 copy-start
  149.8 3.0 %copy-start.3 = (bf16[4,4,256,128]{3,2,1,0:T(8,128)(2,1)S(1)}, bf16[4,4,256,128]{3,2,1,0:T(8,128)(2,1)}, u32[]{:S(2)}) copy-start(bf16[4,4,256,128]{3,2,1,0:T(8,128)(2,1)} %get-tuple-element.7) | copy-start | bytes 3145732
Sparse Core Ops, SparseCore 0:
  10.3 43.8 all-gather.1
  85.7 58.9 all-reduce.2
  149.9 51.6 all-reduce.4

commit v2 on v1

--- a/solution.py
+++ b/solution.py
@@ -32,8 +32,8 @@
 
 
 def head_rows(own_blocks, n_glob, scale, row_base, band_ref, glob_ref, q_of, g_of, key_of, value_of,
-              put_att, put_dq, add_key, add_value):
-    for i in range(own_blocks):
+              put_att, put_dq, add_key, add_value, rows):
+    for i in rows:
         row = row_base + i
         offs = [band_ref[row, 1 + m] for m in range(NBAND - 1)]
         chosen = [glob_ref[row, n] for n in range(n_glob)]
@@ -80,37 +80,291 @@
                 add(2 * own_blocks + n, part[at:at + BLK])
 
 
-def local_kernel(own_blocks, n_glob, scale, band_ref, glob_ref, q_ref, g_ref, kv_ref, att_ref, dq_ref, grads_ref,
-                 acc_ref):
-    row_base = lax.axis_index("ctx") * own_blocks
+def fused_kernel(own, n_glob, owner_step, ctx_count, bits, scale, band_ref, glob_ref, q_ref, g_ref, kv_ref,
+                 att_ref, dq_ref, out_ref,
+                 seen, acc, acc_own, parts, paired, halves, returned, farback, totals, swapped,
+                 near_s, near_r, far_s, far_r, pair_s, pair_r, farpair_s, farpair_r,
+                 one_s, one_r, farone_s, farone_r, back_s, back_r, farback_s, farback_r,
+                 two_s, two_r, three_s, three_r):
+    heads = kv_ref.shape[1]
+    p, s, parity = lax.axis_index("ctx"), lax.axis_index("section"), lax.axis_index("tp") % 2
+
+    def other(j):
+        bit = (1 << (j % bits)) * (1 - parity) + (1 << ((j + 1) % bits)) * parity
+        side = (s // bit) % 2
+        return s + bit * (1 - 2 * side), side
+
+    mate, role = other(0)
+    has_prev, has_next = p > 0, p < ctx_count - 1
+    index = p // owner_step
+
+    def owns(at):
+        return jnp.logical_and(at % owner_step == 0, at // owner_step < n_glob)
+
+    def sends_far(d):
+        return jnp.logical_and(owns(p), p + d < ctx_count)
+
+    def gets_far(d):
+        return jnp.logical_and(p - d >= 0, owns(p - d + (p - d < 0) * ctx_count * owner_step))
+
+    spans = range(2, ctx_count)
+
+    def is_far(n):
+        return p >= n * owner_step + 2
+
+    def is_next(n):
+        return p == n * owner_step + 1
+
+    def copy(src, dst, ss, rs, axis, to):
+        return pltpu.make_async_remote_copy(src_ref=src, dst_ref=dst, send_sem=ss, recv_sem=rs,
+                                            device_id={axis: to}, device_id_type=pl.DeviceIdType.MESH)
+
+    bar = pltpu.get_barrier_semaphore()
+    links = [(has_prev, "ctx", p - 1), (has_next, "ctx", p + 1)]
+    for d in spans:
+        links += [(sends_far(d), "ctx", p + d), (gets_far(d), "ctx", p - d)]
+    for j in range(bits):
+        pl.semaphore_signal(bar, inc=1, device_id={"section": other(j)[0]}, device_id_type=pl.DeviceIdType.MESH)
+    for cond, axis, to in links:
+        @pl.when(cond)
+        def _(axis=axis, to=to):
+            pl.semaphore_signal(bar, inc=1, device_id={axis: to}, device_id_type=pl.DeviceIdType.MESH)
+    peers = bits
+    for cond, _, _ in links:
+        peers = peers + jnp.where(cond, 1, 0)
+    pl.semaphore_wait(bar, peers)
+
+    def near_copy(h):
+        return copy(kv_ref.at[role, h], seen.at[role, h, pl.ds(0, own)], near_s.at[h], near_r.at[h], "ctx", p + 1)
+
+    def far_copy(h, d):
+        return copy(kv_ref.at[role, h, 0], seen.at[role, h, own + index], far_s.at[h, d], far_r.at[h, index],
+                    "ctx", p + d)
+
+    def far_arrival(h, n):
+        return copy(kv_ref.at[role, h, 0], seen.at[role, h, own + n], far_s.at[h, 0], far_r.at[h, n], "ctx", p)
+
+    def pair_copy(h, half):
+        blocks = seen.at[half, h, pl.ds(0, own)]
+        return copy(blocks, blocks, pair_s.at[h], pair_r.at[h], "section", mate)
+
+    def farpair_copy(h, n, half):
+        block = seen.at[half, h, own + n]
+        return copy(block, block, farpair_s.at[h, n], farpair_r.at[h, n], "section", mate)
+
+    def one_copy(h, src_half):
+        return copy(parts.at[src_half, h, pl.ds(0, 2 * own)], paired.at[h, pl.ds(0, 2 * own)],
+                    one_s.at[h], one_r.at[h], "section", mate)
+
+    def farone_copy(h, n, src_half):
+        return copy(parts.at[src_half, h, 2 * own + n], paired.at[h, 2 * own + n],
+                    farone_s.at[h, n], farone_r.at[h, n], "section", mate)
+
+    def back_copy(h):
+        return copy(halves.at[h, pl.ds(0, own)], returned.at[h], back_s.at[h], back_r.at[h], "ctx", p - 1)
+
+    def farback_copy(h, n):
+        return copy(halves.at[h, 2 * own + n], farback.at[h, p - n * owner_step], farback_s.at[h, n],
+                    farback_r.at[h, p - n * owner_step], "ctx", n * owner_step)
+
+    def farback_arrival(h, d):
+        return copy(halves.at[h, 2 * own], farback.at[h, d], farback_s.at[h, 0], farback_r.at[h, d], "ctx", p)
+
+    def two_copy(h, j):
+        return copy(totals.at[j, h], swapped.at[j, h], two_s.at[j, h], two_r.at[j, h], "section", other(j)[0])
+
+    def three_copy(h, half):
+        return copy(out_ref.at[half, h], out_ref.at[half, h], three_s.at[h], three_r.at[h], "section", mate)
+
+    for h in range(heads):
+        @pl.when(has_next)
+        def _(h=h):
+            near_copy(h).start()
+        for d in spans:
+            @pl.when(sends_far(d))
+            def _(h=h, d=d):
+                far_copy(h, d).start()
+
+    @pl.when(jnp.logical_not(has_prev))
+    def _():
+        seen[:, :, :own] = jnp.zeros_like(seen[:, :, :own])
+    for n in range(n_glob):
+        @pl.when(p < n * owner_step + 1)
+        def _(n=n):
+            seen[:, :, own + n] = jnp.zeros_like(seen[:, :, own + n])
+
+    def pass_on(h):
+        @pl.when(has_prev)
+        def _():
+            near_copy(h).wait_recv()
+            pair_copy(h, role).start()
+        for n in range(n_glob):
+            @pl.when(is_far(n))
+            def _(n=n):
+                far_arrival(h, n).wait_recv()
+                farpair_copy(h, n, role).start()
+
+    def arrived(h):
+        @pl.when(has_prev)
+        def _():
+            pair_copy(h, 1 - role).wait_recv()
+        for n in range(n_glob):
+            @pl.when(is_far(n))
+            def _(n=n):
+                farpair_copy(h, n, 1 - role).wait_recv()
+
+            @pl.when(is_next(n))
+            def _(n=n):
+                seen[:, h, own + n] = seen[:, h, 0]
+
     touched = set()
 
     def add_to(which):
         def add(slot, part):
             if (which, slot) in touched:
-                acc_ref[which, slot] += part
+                acc[which, slot] += part
             else:
-                acc_ref[which, slot] = part
+                acc[which, slot] = part
                 touched.add((which, slot))
         return add
 
-    def put_att(i, x):
-        att_ref[0, i] = x
-
-    def put_dq(i, x):
-        dq_ref[0, i] = x
-
-    head_rows(own_blocks, n_glob, scale, row_base, band_ref, glob_ref,
-              lambda i: q_ref[0, i], lambda i: g_ref[0, i],
-              lambda slot: kv_ref[0, 0, slot], lambda slot: kv_ref[1, 0, slot],
-              put_att, put_dq, add_to(0), add_to(1))
-    grads_ref[:, 0] = acc_ref[...].astype(grads_ref.dtype)
-
-
-def passed_along(shard, axis, by):
-    count = lax.axis_size(axis)
-    pairs = [(i, i + by) for i in range(count) if 0 <= i + by < count]
-    return lax.ppermute(shard, axis, pairs)
+    def block_of(which, h):
+        def get(slot):
+            if slot < own:
+                return seen[which, h, slot]
+            if slot < 2 * own:
+                return kv_ref[which, h, slot - own]
+            return seen[which, h, slot - own]
+        return get
+
+    def compute(h, rows):
+        def put_att(i, x):
+            att_ref[h, i] = x
+
+        def put_dq(i, x):
+            dq_ref[h, i] = x
+
+        head_rows(own, n_glob, scale, p * own, band_ref, glob_ref, lambda i: q_ref[h, i], lambda i: g_ref[h, i],
+                  block_of(0, h), block_of(1, h), put_att, put_dq, add_to(0), add_to(1), rows)
+
+    def send_parts(h):
+        for n in range(n_glob):
+            @pl.when(is_next(n))
+            def _(n=n):
+                acc[:, 0] += acc[:, 2 * own + n]
+        parts[:, h] = acc[...].astype(parts.dtype)
+        one_copy(h, 1 - role).start()
+        for n in range(n_glob):
+            @pl.when(is_far(n))
+            def _(n=n):
+                farone_copy(h, n, 1 - role).start()
+
+    def wide(x):
+        return x.astype(jnp.float32)
+
+    def send_back(h):
+        one_copy(h, role).wait_recv()
+        both = pl.ds(0, 2 * own)
+        halves[h, both] = (wide(parts[role, h, both]) + wide(paired[h, both])).astype(halves.dtype)
+
+        @pl.when(has_prev)
+        def _():
+            back_copy(h).start()
+        for n in range(n_glob):
+            @pl.when(is_far(n))
+            def _(n=n):
+                farone_copy(h, n, role).wait_recv()
+                at = 2 * own + n
+                halves[h, at] = (wide(parts[role, h, at]) + wide(paired[h, at])).astype(halves.dtype)
+                farback_copy(h, n).start()
+
+    def swap(h):
+        mine = pl.ds(own, own)
+        total = acc_own
+        total[...] = wide(halves[h, mine])
+
+        @pl.when(has_next)
+        def _():
+            back_copy(h).wait_recv()
+            total[...] += wide(returned[h])
+        for d in spans:
+            @pl.when(sends_far(d))
+            def _(d=d):
+                farback_arrival(h, d).wait_recv()
+                total[0] += wide(farback[h, d])
+        totals[1, h] = total[...].astype(totals.dtype)
+        two_copy(h, 1).start()
+
+    def spread(h):
+        for j in range(1, bits):
+            two_copy(h, j).wait_recv()
+            result = (wide(totals[j, h]) + wide(swapped[j, h])).astype(totals.dtype)
+            if j + 1 < bits:
+                totals[j + 1, h] = result
+                two_copy(h, j + 1).start()
+            else:
+                out_ref[role, h] = result
+        three_copy(h, role).start()
+
+    pass_on(0)
+
+    def step(h, carry):
+        @pl.when(h + 1 < heads)
+        def _():
+            pass_on(h + 1)
+
+        @pl.when(h >= 3)
+        def _():
+            spread(h - 3)
+
+        @pl.when(jnp.logical_and(h >= 2, h < heads + 2))
+        def _():
+            swap(h - 2)
+
+        @pl.when(h < heads)
+        def _():
+            arrived(h)
+            compute(h, range(own // 2))
+
+        @pl.when(jnp.logical_and(h >= 1, h < heads + 1))
+        def _():
+            send_back(h - 1)
+
+        @pl.when(h < heads)
+        def _():
+            compute(h, range(own // 2, own))
+            send_parts(h)
+        return carry
+
+    lax.fori_loop(0, heads + 3, step, 0)
+
+    def finish(h, carry):
+        @pl.when(has_next)
+        def _():
+            near_copy(h).wait_send()
+        for d in spans:
+            @pl.when(sends_far(d))
+            def _(d=d):
+                far_copy(h, d).wait_send()
+
+        @pl.when(has_prev)
+        def _():
+            pair_copy(h, role).wait_send()
+            back_copy(h).wait_send()
+        one_copy(h, 1 - role).wait_send()
+        for n in range(n_glob):
+            @pl.when(is_far(n))
+            def _(n=n):
+                farpair_copy(h, n, role).wait_send()
+                farone_copy(h, n, 1 - role).wait_send()
+                farback_copy(h, n).wait_send()
+        for j in range(1, bits):
+            two_copy(h, j).wait_send()
+        three_copy(h, role).wait_send()
+        three_copy(h, 1 - role).wait_recv()
+        return carry
+
+    lax.fori_loop(0, heads, finish, 0)
 
 
 def rows_first(x, own_blocks):
@@ -127,44 +381,48 @@
 
 def shards(queries, key_states, value_states, out_grad, band_offsets, global_blocks):
     tok, heads, group, dim = queries.shape
-    own_blocks = tok // BLK
-    ctx_count = lax.axis_size("ctx")
-    all_blocks = own_blocks * ctx_count
+    own = tok // BLK
+    ctx_count, sections = lax.axis_size("ctx"), lax.axis_size("section")
+    bits = sections.bit_length() - 1
+    all_blocks = own * ctx_count
     stride_blocks = all_blocks // NGLOB
-    stride_devices = stride_blocks // own_blocks
-    n_glob = global_count(all_blocks, stride_blocks, own_blocks)
-    position = lax.axis_index("ctx")
-    scale = dim ** (-0.5)
-    q, g = rows_first(queries, own_blocks), rows_first(out_grad, own_blocks)
-    own = jnp.stack([key_states, value_states]).transpose(0, 2, 1, 3).reshape(2, heads, own_blocks, BLK, dim)
-    earlier = passed_along(own, "ctx", 1)
-    firsts = lax.all_gather(own[:, :, 0], "ctx", axis=2)[:, :, ::stride_devices][:, :, :n_glob]
-    stacked = jnp.concatenate([earlier, own, firsts], axis=2)
-    slots = 2 * own_blocks + n_glob
-    smem = pl.BlockSpec(memory_space=pltpu.SMEM)
-    row_spec = pl.BlockSpec((1, own_blocks, group * BLK, dim), lambda h: (h, 0, 0, 0))
-    slot_spec = pl.BlockSpec((2, 1, slots, BLK, dim), lambda h: (0, h, 0, 0, 0))
-    att, dq, grads = pl.pallas_call(
-        functools.partial(local_kernel, own_blocks, n_glob, scale),
-        grid=(heads,),
-        in_specs=[smem, smem, row_spec, row_spec, slot_spec],
-        out_specs=[row_spec, row_spec, slot_spec],
+    n_glob = global_count(all_blocks, stride_blocks, own)
+    slots = 2 * own + n_glob
+    q, g = rows_first(queries, own), rows_first(out_grad, own)
+    kv = jnp.stack([key_states, value_states]).transpose(0, 2, 1, 3).reshape(2, heads, own, BLK, dim)
+    smem, vmem = pl.BlockSpec(memory_space=pltpu.SMEM), pl.BlockSpec(memory_space=pltpu.VMEM)
+
+    def low(*lead):
+        return pltpu.VMEM((*lead, BLK, dim), jnp.bfloat16)
+
+    def sems(*dims):
+        return [pltpu.SemaphoreType.DMA(dims)] * 2
+
+    att, dq, totals = pl.pallas_call(
+        functools.partial(fused_kernel, own, n_glob, stride_blocks // own, ctx_count, bits, dim ** (-0.5)),
+        in_specs=[smem, smem, vmem, vmem, vmem],
+        out_specs=[vmem, vmem, vmem],
         out_shape=[
             jax.ShapeDtypeStruct(q.shape, jnp.bfloat16),
             jax.ShapeDtypeStruct(q.shape, jnp.float32),
-            jax.ShapeDtypeStruct((2, heads, slots, BLK, dim), jnp.bfloat16),
+            jax.ShapeDtypeStruct(kv.shape, jnp.bfloat16),
         ],
-        scratch_shapes=[pltpu.VMEM((2, slots, BLK, dim), jnp.float32)],
-        compiler_params=pltpu.CompilerParams(vmem_limit_bytes=56 * 2**20),
-    )(band_offsets, global_blocks, q, g, stacked)
-    back = passed_along(grads[:, :, :own_blocks], "ctx", -1)
-    own_grads = grads[:, :, own_blocks:2 * own_blocks].astype(jnp.float32) + back.astype(jnp.float32)
-    summed = lax.psum(grads[:, :, 2 * own_blocks:], "ctx").astype(jnp.float32)
-    mine = (jnp.arange(n_glob) * stride_devices == position)[None, None, :, None, None]
-    first = jnp.sum(jnp.where(mine, summed, 0.0), axis=2)
-    own_grads = jnp.concatenate([own_grads[:, :, :1] + first[:, :, None], own_grads[:, :, 1:]], axis=2)
-    totals = lax.psum(own_grads.astype(jnp.bfloat16), "section").astype(jnp.float32)
-    totals = totals.reshape(2, heads, tok, dim).transpose(0, 2, 1, 3)
+        scratch_shapes=[
+            low(2, heads, own + n_glob),
+            pltpu.VMEM((2, slots, BLK, dim), jnp.float32),
+            pltpu.VMEM((own, BLK, dim), jnp.float32),
+            low(2, heads, slots), low(heads, slots), low(heads, slots), low(heads, own), low(heads, ctx_count),
+            low(bits, heads, own), low(bits, heads, own),
+            *sems(heads), pltpu.SemaphoreType.DMA((heads, ctx_count)), pltpu.SemaphoreType.DMA((heads, n_glob)),
+            *sems(heads), *sems(heads, n_glob),
+            *sems(heads), *sems(heads, n_glob),
+            *sems(heads), pltpu.SemaphoreType.DMA((heads, n_glob)), pltpu.SemaphoreType.DMA((heads, ctx_count)),
+            *sems(bits, heads), *sems(heads),
+        ],
+        compiler_params=pltpu.CompilerParams(
+            vmem_limit_bytes=56 * 2**20, collective_id=0, has_side_effects=True),
+    )(band_offsets, global_blocks, q, g, kv)
+    totals = totals.reshape(2, heads, tok, dim).transpose(0, 2, 1, 3).astype(jnp.float32)
     return rows_back(att, group), rows_back(dq, group), totals[0], totals[1]
 
 

time: 212 us -> 94.1 us (0.44)
  waiting for transfers between devices: 140 us -> 0 us
  Pallas kernels: 22.4 us -> 75.5 us
  between operations: 13.9 us -> 0.69 us
  other arithmetic: 9.75 us -> 0.94 us
  starting transfers between devices: 7.53 us -> 0 us
    psum x2 -> x0, waiting for transfers between devices: 106 us -> none  [the longest x1 58.8 us: shards(): summed = lax.psum(grads[:, :, 2 * own_blocks:], 'ctx').astype(jnp.float32)]
    pallas_call x1, Pallas kernels: 22.4 us -> 75.5 us  [shards(): pl.pallas_call(functools.partial(fused_kernel, own, n_glob, stride_blocks...]
    all_gather x1 -> x0, waiting for transfers between devices: 34.2 us -> none  [shards(): lax.all_gather(own[:, :, 0], 'ctx', axis=2)[:, :, ::stride_devices]]
    ppermute x2 -> x0, starting transfers between devices: 7.23 us -> none  [passed_along(): return lax.ppermute(shard, axis, pairs)]
    slice x6 -> x0, local copies, waits for them, and re-layouts: 5.12 us -> none  [the longest x1 2.09 us: shards(): summed = lax.psum(grads[:, :, 2 * own_blocks:], 'ctx').astype(jnp.float32)]
    concatenate x2 -> x0, other arithmetic: 3.24 us -> none  [the longest x1 3.15 us: shards(): stacked = jnp.concatenate([earlier, own, firsts], axis=2)]
  transfers between devices with their start and end apart: 5 -> 0, of which waited for: 4 -> 0; matrix products, arithmetic and copies ran while one was open for 6% -> 0% of each run, Pallas kernels for 0% -> 0%
where the time goes in v2:
time: 94.1 us; the launch traced here: 93.9 us
  Pallas kernels  75.5 us (80%)
  local copies, waits for them, and re-layouts  16.7 us (18%)
    pallas_call x1, Pallas kernels, shards(): pl.pallas_call(functools.partial(fused_kernel, own, n_glob, stride_blocks...  75.5 us
    transpose x2, local copies, waits for them, and re-layouts, rows_back(): jnp.transpose(x, (1, 3, 0, 2, 4))  6.36 us
    reshape x2, local copies, waits for them, and re-layouts, rows_first(): x = x.reshape(own_blocks, BLK, heads, group, dim)  3.66 us
    unnamed x12, local copies, waits for them, and re-layouts  2.81 us

profile of v2, /device:TPU:0, one launch (start us, length us, event | category | flops | bytes accessed | tf_op | source)
XLA Modules:
  0.0 93.9 jit_solution(11613947986515780857)
XLA Ops:
  0.6 0.0 copy-start.3
  0.6 0.0 copy-start.4
  0.7 1.4 %copy.13.band_ref = s32[16,3]{1,0:T(8,128)} copy(s32[16,3]{0,1:T(4,128)} %param.10) | data formatting | bytes 384 | tf_op args[4]
  2.1 1.4 %copy.14.glob_ref = s32[16,4]{1,0:T(8,128)} copy(s32[16,4]{0,1:T(4,128)} %param.11) | data formatting | bytes 512 | tf_op args[5]
  3.4 2.4 %copy.10 = bf16[4,128,4,2,128]{4,1,3,0,2:T(8,128)(2,1)} copy(bf16[4,128,4,2,128]{4,3,2,1,0:T(2,128)(2,1)} %bitcast.37) | data formatting | bytes 2097152 | tf_op jit(solution)/shard_map/reshape | solution.py:372
  5.9 0.0 copy-done.3
  5.9 0.0 copy-done.4
  5.9 0.0 copy-start.2
  5.9 0.7 maximum_bitcast_fusion
  6.6 1.1 %copy.12 = bf16[2,4,512,128]{3,2,1,0:T(8,128)(2,1)} copy(bf16[2,4,512,128]{3,1,2,0:T(4,128)(2,1)S(1)} %maximum_bitcast_fusion) | data formatting | bytes 2097152 | tf_op jit(solution)/shard_map/transpose | solution.py:392
  7.7 0.0 copy-done.2
  7.8 1.2 %copy.11 = bf16[4,128,4,2,128]{4,1,3,0,2:T(8,128)(2,1)} copy(bf16[4,128,4,2,128]{4,3,2,1,0:T(2,128)(2,1)S(1)} %bitcast.38) | data formatting | bytes 2097152 | tf_op jit(solution)/shard_map/reshape | solution.py:372
  9.0 75.5 %shard_map.93 = (bf16[4,4,256,128]{3,2,1,0:T(8,128)(2,1)}, f32[4,4,256,128]{3,2,1,0:T(8,128)}, bf16[2,4,4,128,128]{4,3,2,1,0:T(8,128)(2,1)}) custom-call(s32[16,3]{1,0:T(8,128)} %copy.13.band_ref, s32[16,4]{1,0:T(8,128)} %copy.14.glob_ref, bf16[4,4,256,128]{3,2,1,0:T(8,128)(2,1)} %bitcast.32, bf16[4,4,256,128]{3,2,1,0:T(8,128)(2,1)} %bitcast.34, ...), custom_call_target="tpu_custom_call" | custom-call | tf_op jit(solution)/shard_map/pallas_call | solution.py:401
  84.5 0.0 copy-start
  84.5 3.4 %copy.15 = bf16[4,128,4,2,128]{4,3,2,1,0:T(2,128)(2,1)} copy(bf16[4,128,4,2,128]{4,1,3,0,2:T(8,128)(2,1)} %bitcast.40) | data formatting | bytes 2097152 | tf_op jit(solution)/shard_map/transpose | solution.py:379
  88.0 0.0 copy-done
  88.0 0.0 copy-start.1
  88.0 2.9 %copy.16 = f32[4,128,4,2,128]{4,3,2,1,0:T(2,128)} copy(f32[4,128,4,2,128]{4,1,3,0,2:T(8,128)S(1)} %bitcast.36) | data formatting | bytes 4194304 | tf_op jit(solution)/shard_map/transpose | solution.py:379
  90.9 0.0 copy-done.1
  90.9 0.2 bitcast_convert_fusion
  91.1 1.4 %copy.19 = f32[2,4,512,128]{3,1,2,0:T(4,128)S(1)} copy(f32[2,4,512,128]{3,2,1,0:T(8,128)S(1)} %bitcast_convert_fusion) | data formatting | bytes 4194304 | tf_op jit(solution)/shard_map/convert_element_type | solution.py:425
  92.5 1.5 %slice_bitcast_fusion = (f32[512,4,128]{2,1,0:T(4,128)}, f32[512,4,128]{2,1,0:T(4,128)}) fusion(f32[2,512,4,128]{3,2,1,0:T(4,128)S(1)} %bitcast.31), kind=kLoop, calls=%fused_computation.1 | loop fusion | bytes 4194304 | tf_op jit(solution)/shard_map/squeeze | solution.py:426
Async XLA Ops:
  0.6 5.3 %copy-start.3 = (bf16[512,4,128]{2,1,0:T(4,128)(2,1)S(1)}, bf16[512,4,128]{2,1,0:T(4,128)(2,1)}, u32[]{:S(2)}) copy-start(bf16[512,4,128]{2,1,0:T(4,128)(2,1)} %param.8) | copy-start | bytes 1572868
  0.6 5.3 %copy-start.4 = (bf16[512,4,128]{2,1,0:T(4,128)(2,1)S(1)}, bf16[512,4,128]{2,1,0:T(4,128)(2,1)}, u32[]{:S(2)}) copy-start(bf16[512,4,128]{2,1,0:T(4,128)(2,1)} %param.7) | copy-start | bytes 1572868
  5.9 1.9 %copy-start.2 = (bf16[512,4,2,128]{3,2,1,0:T(2,128)(2,1)S(1)}, bf16[512,4,2,128]{3,2,1,0:T(2,128)(2,1)}, u32[]{:S(2)}) copy-start(bf16[512,4,2,128]{3,2,1,0:T(2,128)(2,1)} %param.9) | copy-start | bytes 3145732
  84.5 3.4 %copy-start = (f32[4,4,256,128]{3,2,1,0:T(8,128)S(1)}, f32[4,4,256,128]{3,2,1,0:T(8,128)}, u32[]{:S(2)}) copy-start(f32[4,4,256,128]{3,2,1,0:T(8,128)} %get-tuple-element.8) | copy-start | bytes 6291460
  88.0 2.9 %copy-start.1 = (bf16[2,4,4,128,128]{4,3,2,1,0:T(8,128)(2,1)S(1)}, bf16[2,4,4,128,128]{4,3,2,1,0:T(8,128)(2,1)}, u32[]{:S(2)}) copy-start(bf16[2,4,4,128,128]{4,3,2,1,0:T(8,128)(2,1)} %get-tuple-element.9) | copy-start | bytes 3145732

commit v3 on v2

--- a/solution.py
+++ b/solution.py
@@ -35,8 +35,8 @@
               put_att, put_dq, add_key, add_value, rows):
     for i in rows:
         row = row_base + i
-        offs = [band_ref[row, 1 + m] for m in range(NBAND - 1)]
-        chosen = [glob_ref[row, n] for n in range(n_glob)]
+        offs = [band_ref[1 + m, row] for m in range(NBAND - 1)]
+        chosen = [glob_ref[n, row] for n in range(n_glob)]
         q, g = q_of(i), g_of(i)
 
         def selected(block_of):
@@ -64,7 +64,7 @@
         weights = probs * (1.0 / jnp.sum(probs, axis=0, keepdims=True))
         low = weights.astype(jnp.bfloat16)
         att = dot_tn(values, low).astype(jnp.bfloat16).astype(jnp.float32)
-        put_att(i, att.T.astype(jnp.bfloat16))
+        put_att(i, att.T)
         dots = jnp.sum(g.astype(jnp.float32).T * att, axis=0, keepdims=True)
         ds = (weights * (dot_nt(values, g) - dots)).astype(jnp.bfloat16)
         put_dq(i, (dot_tn(keys, ds) * scale).T)
@@ -80,13 +80,19 @@
                 add(2 * own_blocks + n, part[at:at + BLK])
 
 
-def fused_kernel(own, n_glob, owner_step, ctx_count, bits, scale, band_ref, glob_ref, q_ref, g_ref, kv_ref,
-                 att_ref, dq_ref, out_ref,
-                 seen, acc, acc_own, parts, paired, halves, returned, farback, totals, swapped,
+def fused_kernel(own, n_glob, owner_step, ctx_count, bits, scale, group, band_ref, glob_ref, q_ref, g_ref,
+                 key_ref, value_ref, att_ref, dq_ref, dkey_ref, dvalue_ref,
+                 kv_wide, kv_ref, q_wide, g_wide, att_wide, out_ref, seen, acc, acc_own, parts, paired, halves, returned, farback, totals, swapped,
                  near_s, near_r, far_s, far_r, pair_s, pair_r, farpair_s, farpair_r,
-                 one_s, one_r, farone_s, farone_r, back_s, back_r, farback_s, farback_r,
+                 one_s, one_r, own_s, own_r, farone_s, farone_r, back_s, back_r, farback_s, farback_r,
                  two_s, two_r, three_s, three_r):
-    heads = kv_ref.shape[1]
+    heads, dim = kv_ref.shape[1], kv_ref.shape[-1]
+    tok, lanes = own * BLK, heads * group
+
+    for which, ref in enumerate((key_ref, value_ref)):
+        kv_wide[...] = ref[...].astype(jnp.float32)
+        for h in range(heads):
+            kv_ref[which, h] = kv_wide[pl.ds(h, tok, stride=heads), :].astype(kv_ref.dtype).reshape(own, BLK, dim)
     p, s, parity = lax.axis_index("ctx"), lax.axis_index("section"), lax.axis_index("tp") % 2
 
     def other(j):
@@ -153,8 +159,12 @@
         return copy(block, block, farpair_s.at[h, n], farpair_r.at[h, n], "section", mate)
 
     def one_copy(h, src_half):
-        return copy(parts.at[src_half, h, pl.ds(0, 2 * own)], paired.at[h, pl.ds(0, 2 * own)],
+        return copy(parts.at[src_half, h, pl.ds(0, own)], paired.at[h, pl.ds(0, own)],
                     one_s.at[h], one_r.at[h], "section", mate)
+
+    def own_copy(h, src_half):
+        return copy(parts.at[src_half, h, pl.ds(own, own)], paired.at[h, pl.ds(own, own)],
+                    own_s.at[h], own_r.at[h], "section", mate)
 
     def farone_copy(h, n, src_half):
         return copy(parts.at[src_half, h, 2 * own + n], paired.at[h, 2 * own + n],
@@ -238,13 +248,21 @@
         return get
 
     def compute(h, rows):
+        def spots(i):
+            return [pl.ds(i * BLK * lanes + h * group + n, BLK, stride=lanes) for n in range(group)]
+
+        def rows_of(ref, i):
+            return jnp.concatenate([ref[at, :] for at in spots(i)], axis=0).astype(jnp.bfloat16)
+
         def put_att(i, x):
-            att_ref[h, i] = x
+            for n, at in enumerate(spots(i)):
+                att_wide[at, :] = x[n * BLK:(n + 1) * BLK]
 
         def put_dq(i, x):
-            dq_ref[h, i] = x
-
-        head_rows(own, n_glob, scale, p * own, band_ref, glob_ref, lambda i: q_ref[h, i], lambda i: g_ref[h, i],
+            for n, at in enumerate(spots(i)):
+                dq_ref[at, :] = x[n * BLK:(n + 1) * BLK]
+
+        head_rows(own, n_glob, scale, p * own, band_ref, glob_ref, lambda i: rows_of(q_wide, i), lambda i: rows_of(g_wide, i),
                   block_of(0, h), block_of(1, h), put_att, put_dq, add_to(0), add_to(1), rows)
 
     def send_parts(h):
@@ -258,13 +276,14 @@
             @pl.when(is_far(n))
             def _(n=n):
                 farone_copy(h, n, 1 - role).start()
+        own_copy(h, 1 - role).start()
 
     def wide(x):
         return x.astype(jnp.float32)
 
     def send_back(h):
         one_copy(h, role).wait_recv()
-        both = pl.ds(0, 2 * own)
+        both = pl.ds(0, own)
         halves[h, both] = (wide(parts[role, h, both]) + wide(paired[h, both])).astype(halves.dtype)
 
         @pl.when(has_prev)
@@ -277,6 +296,9 @@
                 at = 2 * own + n
                 halves[h, at] = (wide(parts[role, h, at]) + wide(paired[h, at])).astype(halves.dtype)
                 farback_copy(h, n).start()
+        own_copy(h, role).wait_recv()
+        mine = pl.ds(own, own)
+        halves[h, mine] = (wide(parts[role, h, mine]) + wide(paired[h, mine])).astype(halves.dtype)
 
     def swap(h):
         mine = pl.ds(own, own)
@@ -306,6 +328,8 @@
                 out_ref[role, h] = result
         three_copy(h, role).start()
 
+    q_wide[...] = q_ref[...].astype(jnp.float32)
+    g_wide[...] = g_ref[...].astype(jnp.float32)
     pass_on(0)
 
     def step(h, carry):
@@ -325,6 +349,10 @@
         def _():
             arrived(h)
             compute(h, range(own // 2))
+
+        @pl.when(h == heads)
+        def _():
+            att_ref[...] = att_wide[...].astype(att_ref.dtype)
 
         @pl.when(jnp.logical_and(h >= 1, h < heads + 1))
         def _():
@@ -352,6 +380,7 @@
             pair_copy(h, role).wait_send()
             back_copy(h).wait_send()
         one_copy(h, 1 - role).wait_send()
+        own_copy(h, 1 - role).wait_send()
         for n in range(n_glob):
             @pl.when(is_far(n))
             def _(n=n):
@@ -362,21 +391,11 @@
             two_copy(h, j).wait_send()
         three_copy(h, role).wait_send()
         three_copy(h, 1 - role).wait_recv()
+        for which, ref in enumerate((dkey_ref, dvalue_ref)):
+            ref[pl.ds(h, tok, stride=heads), :] = wide(out_ref[which, h]).reshape(tok, dim)
         return carry
 
     lax.fori_loop(0, heads, finish, 0)
-
-
-def rows_first(x, own_blocks):
-    tok, heads, group, dim = x.shape
-    x = x.reshape(own_blocks, BLK, heads, group, dim)
-    return jnp.transpose(x, (2, 0, 3, 1, 4)).reshape(heads, own_blocks, group * BLK, dim)
-
-
-def rows_back(x, group):
-    heads, own_blocks, _, dim = x.shape
-    x = x.reshape(heads, own_blocks, group, BLK, dim)
-    return jnp.transpose(x, (1, 3, 0, 2, 4)).reshape(own_blocks * BLK, heads, group, dim)
 
 
 def shards(queries, key_states, value_states, out_grad, band_offsets, global_blocks):
@@ -388,8 +407,7 @@
     stride_blocks = all_blocks // NGLOB
     n_glob = global_count(all_blocks, stride_blocks, own)
     slots = 2 * own + n_glob
-    q, g = rows_first(queries, own), rows_first(out_grad, own)
-    kv = jnp.stack([key_states, value_states]).transpose(0, 2, 1, 3).reshape(2, heads, own, BLK, dim)
+    flat, narrow = (tok * heads * group, dim), (tok * heads, dim)
     smem, vmem = pl.BlockSpec(memory_space=pltpu.SMEM), pl.BlockSpec(memory_space=pltpu.VMEM)
 
     def low(*lead):
@@ -398,16 +416,20 @@
     def sems(*dims):
         return [pltpu.SemaphoreType.DMA(dims)] * 2
 
-    att, dq, totals = pl.pallas_call(
-        functools.partial(fused_kernel, own, n_glob, stride_blocks // own, ctx_count, bits, dim ** (-0.5)),
-        in_specs=[smem, smem, vmem, vmem, vmem],
-        out_specs=[vmem, vmem, vmem],
+    att, dq, dkey, dvalue = pl.pallas_call(
+        functools.partial(fused_kernel, own, n_glob, stride_blocks // own, ctx_count, bits, dim ** (-0.5), group),
+        in_specs=[smem, smem, vmem, vmem, vmem, vmem],
+        out_specs=[vmem, vmem, vmem, vmem],
         out_shape=[
-            jax.ShapeDtypeStruct(q.shape, jnp.bfloat16),
-            jax.ShapeDtypeStruct(q.shape, jnp.float32),
-            jax.ShapeDtypeStruct(kv.shape, jnp.bfloat16),
+            jax.ShapeDtypeStruct(flat, jnp.bfloat16),
+            jax.ShapeDtypeStruct(flat, jnp.float32),
+            jax.ShapeDtypeStruct(narrow, jnp.float32),
+            jax.ShapeDtypeStruct(narrow, jnp.float32),
         ],
         scratch_shapes=[
+            pltpu.VMEM(narrow, jnp.float32), low(2, heads, own),
+            pltpu.VMEM(flat, jnp.float32), pltpu.VMEM(flat, jnp.float32), pltpu.VMEM(flat, jnp.float32),
+            low(2, heads, own),
             low(2, heads, own + n_glob),
             pltpu.VMEM((2, slots, BLK, dim), jnp.float32),
             pltpu.VMEM((own, BLK, dim), jnp.float32),
@@ -415,15 +437,16 @@
             low(bits, heads, own), low(bits, heads, own),
             *sems(heads), pltpu.SemaphoreType.DMA((heads, ctx_count)), pltpu.SemaphoreType.DMA((heads, n_glob)),
             *sems(heads), *sems(heads, n_glob),
-            *sems(heads), *sems(heads, n_glob),
+            *sems(heads), *sems(heads), *sems(heads, n_glob),
             *sems(heads), pltpu.SemaphoreType.DMA((heads, n_glob)), pltpu.SemaphoreType.DMA((heads, ctx_count)),
             *sems(bits, heads), *sems(heads),
         ],
         compiler_params=pltpu.CompilerParams(
             vmem_limit_bytes=56 * 2**20, collective_id=0, has_side_effects=True),
-    )(band_offsets, global_blocks, q, g, kv)
-    totals = totals.reshape(2, heads, tok, dim).transpose(0, 2, 1, 3).astype(jnp.float32)
-    return rows_back(att, group), rows_back(dq, group), totals[0], totals[1]
+    )(band_offsets.T, global_blocks.T, queries.reshape(flat), out_grad.reshape(flat),
+      key_states.reshape(narrow), value_states.reshape(narrow))
+    return (att.reshape(queries.shape), dq.reshape(queries.shape), dkey.reshape(key_states.shape),
+            dvalue.reshape(key_states.shape))
 
 
 def solution(mesh):

time: 94.1 us -> 82.8 us (0.88)
  local copies, waits for them, and re-layouts: 16.7 us -> 6.97 us
    transpose x3 -> x0, local copies, waits for them, and re-layouts: 7.47 us -> none  [the longest x2 6.36 us: rows_back(): jnp.transpose(x, (1, 3, 0, 2, 4))]
    unnamed x12 -> x10, local copies, waits for them, and re-layouts: 2.81 us -> 6.97 us
    reshape x2 -> x0, local copies, waits for them, and re-layouts: 3.66 us -> none  [rows_first(): x = x.reshape(own_blocks, BLK, heads, group, dim)]
    squeeze x1 -> x0, local copies, waits for them, and re-layouts: 1.45 us -> none  [shards(): return (rows_back(att, group), rows_back(dq, group), totals[0], totals[1])]
    convert_element_type x1 -> x0, local copies, waits for them, and re-layouts: 1.35 us -> none  [shards(): totals.reshape(2, heads, tok, dim).transpose(0, 2, 1, 3).astype(jnp.float32)]
where the time goes in v3:
time: 82.8 us; the launch traced here: 82.6 us
  Pallas kernels  75 us (91%)
  local copies, waits for them, and re-layouts  6.97 us (8%)
    pallas_call x1, Pallas kernels, shards(): pl.pallas_call(functools.partial(fused_kernel, own, n_glob, stride_blocks...  75 us
    unnamed x10, local copies, waits for them, and re-layouts  6.97 us

profile of v3, /device:TPU:0, one launch (start us, length us, event | category | flops | bytes accessed | tf_op | source)
XLA Modules:
  0.0 82.6 jit_solution(10636433599649345333)
XLA Ops:
  0.6 75.0 %shard_map.93 = (bf16[4096,128]{1,0:T(8,128)(2,1)}, f32[4096,128]{1,0:T(8,128)}, f32[2048,128]{1,0:T(8,128)}, f32[2048,128]{1,0:T(8,128)}) custom-call(s32[3,16]{1,0:T(4,128)} %bitcast.18, s32[4,16]{1,0:T(4,128)} %bitcast.19, bf16[4096,128]{1,0:T(8,128)(2,1)} %bitcast.11, bf16[4096,128]{1,0:T(8,128)(2,1)} %bitcast.12, bf16[2048,128]{1,0:T(8,128)(2,1)} %bitcast.16, ...), custom_call_target="tpu_custom_call" | custom-call | tf_op jit(solution)/shard_map/pallas_call | solution.py:419
  75.7 0.0 copy-start
  75.7 3.1 %copy.14 = bf16[512,4,2,128]{3,2,1,0:T(2,128)(2,1)} copy(bf16[512,4,2,128]{3,2,1,0:T(2,128)(2,1)} %bitcast.15) | data formatting | bytes 2097152
  78.7 0.0 copy-done
  78.7 0.0 copy-start.2
  78.7 0.0 copy-start.1
  78.7 1.3 %copy.15 = f32[512,4,2,128]{3,2,1,0:T(2,128)} copy(f32[512,4,2,128]{3,2,1,0:T(2,128)S(1)} %bitcast.10) | data formatting | bytes 4194304
  80.1 0.6 copy-done.2
  80.7 1.0 %copy.16 = f32[512,4,128]{2,1,0:T(4,128)} copy(f32[512,4,128]{2,1,0:T(4,128)S(1)} %bitcast.14) | data formatting | bytes 2097152
  81.7 0.0 copy-done.1
  81.7 1.0 %copy.17 = f32[512,4,128]{2,1,0:T(4,128)} copy(f32[512,4,128]{2,1,0:T(4,128)S(1)} %bitcast.13) | data formatting | bytes 2097152
Async XLA Ops:
  75.7 3.1 %copy-start = (f32[4096,128]{1,0:T(8,128)S(1)}, f32[4096,128]{1,0:T(8,128)}, u32[]{:S(2)}) copy-start(f32[4096,128]{1,0:T(8,128)} %get-tuple-element.9) | copy-start | bytes 6291460
  78.7 2.0 %copy-start.2 = (f32[2048,128]{1,0:T(8,128)S(1)}, f32[2048,128]{1,0:T(8,128)}, u32[]{:S(2)}) copy-start(f32[2048,128]{1,0:T(8,128)} %get-tuple-element.10) | copy-start | bytes 3145732
  78.7 2.9 %copy-start.1 = (f32[2048,128]{1,0:T(8,128)S(1)}, f32[2048,128]{1,0:T(8,128)}, u32[]{:S(2)}) copy-start(f32[2048,128]{1,0:T(8,128)} %get-tuple-element.11) | copy-start | bytes 3145732

commit v4 on v3

--- a/solution.py
+++ b/solution.py
@@ -333,10 +333,6 @@
     pass_on(0)
 
     def step(h, carry):
-        @pl.when(h + 1 < heads)
-        def _():
-            pass_on(h + 1)
-
         @pl.when(h >= 3)
         def _():
             spread(h - 3)
@@ -349,6 +345,10 @@
         def _():
             arrived(h)
             compute(h, range(own // 2))
+
+        @pl.when(h + 1 < heads)
+        def _():
+            pass_on(h + 1)
 
         @pl.when(h == heads)
         def _():
@@ -442,7 +442,7 @@
             *sems(bits, heads), *sems(heads),
         ],
         compiler_params=pltpu.CompilerParams(
-            vmem_limit_bytes=56 * 2**20, collective_id=0, has_side_effects=True),
+            vmem_limit_bytes=40 * 2**20, collective_id=0, has_side_effects=True),
     )(band_offsets.T, global_blocks.T, queries.reshape(flat), out_grad.reshape(flat),
       key_states.reshape(narrow), value_states.reshape(narrow))
     return (att.reshape(queries.shape), dq.reshape(queries.shape), dkey.reshape(key_states.shape),

time: 82.8 us -> 79.8 us (0.964)
  Pallas kernels: 75 us -> 68.7 us
  local copies, waits for them, and re-layouts: 6.97 us -> 10.1 us
    pallas_call x1, Pallas kernels: 75 us -> 68.7 us  [shards(): pl.pallas_call(functools.partial(fused_kernel, own, n_glob, stride_blocks...]
    unnamed x10 -> x16, local copies, waits for them, and re-layouts: 6.97 us -> 10.1 us
where the time goes in v4:
time: 79.8 us; the launch traced here: 79.5 us
  Pallas kernels  68.7 us (86%)
  local copies, waits for them, and re-layouts  10.1 us (13%)
    pallas_call x1, Pallas kernels, shards(): pl.pallas_call(functools.partial(fused_kernel, own, n_glob, stride_blocks...  68.7 us
    unnamed x16, local copies, waits for them, and re-layouts  10.1 us

profile of v4, /device:TPU:0, one launch (start us, length us, event | category | flops | bytes accessed | tf_op | source)
XLA Modules:
  0.0 79.5 jit_solution(3508405197124567245)
XLA Ops:
  0.6 0.0 copy-start
  0.6 1.2 %copy-done = bf16[512,4,2,128]{3,2,1,0:T(2,128)(2,1)S(1)} copy-done((bf16[512,4,2,128]{3,2,1,0:T(2,128)(2,1)S(1)}, bf16[512,4,2,128]{3,2,1,0:T(2,128)(2,1)}, u32[]{:S(2)}) %copy-start) | copy-done | bytes 1048600
  1.9 0.0 copy-start.1
  1.9 1.2 %copy-done.1 = bf16[512,4,2,128]{3,2,1,0:T(2,128)(2,1)S(1)} copy-done((bf16[512,4,2,128]{3,2,1,0:T(2,128)(2,1)S(1)}, bf16[512,4,2,128]{3,2,1,0:T(2,128)(2,1)}, u32[]{:S(2)}) %copy-start.1) | copy-done | bytes 1048600
  3.1 0.0 copy-start.2
  3.1 1.0 %copy-done.2 = bf16[512,4,128]{2,1,0:T(4,128)(2,1)S(1)} copy-done((bf16[512,4,128]{2,1,0:T(4,128)(2,1)S(1)}, bf16[512,4,128]{2,1,0:T(4,128)(2,1)}, u32[]{:S(2)}) %copy-start.2) | copy-done | bytes 524312
  4.1 0.0 copy-start.3
  4.1 1.0 %copy-done.3 = bf16[512,4,128]{2,1,0:T(4,128)(2,1)S(1)} copy-done((bf16[512,4,128]{2,1,0:T(4,128)(2,1)S(1)}, bf16[512,4,128]{2,1,0:T(4,128)(2,1)}, u32[]{:S(2)}) %copy-start.3) | copy-done | bytes 524312
  5.2 0.0 copy-start.4
  5.2 0.7 copy-done.4
  5.8 0.0 copy-start.5
  5.9 0.7 copy-done.5
  6.5 68.7 %shard_map.93 = (bf16[4096,128]{1,0:T(8,128)(2,1)S(1)}, f32[4096,128]{1,0:T(8,128)S(1)}, f32[2048,128]{1,0:T(8,128)S(1)}, f32[2048,128]{1,0:T(8,128)S(1)}) custom-call(s32[3,16]{1,0:T(4,128)S(1)} %bitcast.18, s32[4,16]{1,0:T(4,128)S(1)} %bitcast.19, bf16[4096,128]{1,0:T(8,128)(2,1)S(1)} %bitcast.11, bf16[4096,128]{1,0:T(8,128)(2,1)S(1)} %bitcast.12, ...), custom_call_target="tpu_custom_call" | custom-call | tf_op jit(solution)/shard_map/pallas_call | solution.py:419
  75.2 1.0 %copy.14 = bf16[512,4,2,128]{3,2,1,0:T(2,128)(2,1)} copy(bf16[512,4,2,128]{3,2,1,0:T(2,128)(2,1)S(1)} %bitcast.15) | data formatting | bytes 2097152
  76.2 1.3 %copy.15 = f32[512,4,2,128]{3,2,1,0:T(2,128)} copy(f32[512,4,2,128]{3,2,1,0:T(2,128)S(1)} %bitcast.10) | data formatting | bytes 4194304
  77.5 1.0 %copy.16 = f32[512,4,128]{2,1,0:T(4,128)} copy(f32[512,4,128]{2,1,0:T(4,128)S(1)} %bitcast.14) | data formatting | bytes 2097152
  78.5 1.0 %copy.17 = f32[512,4,128]{2,1,0:T(4,128)} copy(f32[512,4,128]{2,1,0:T(4,128)S(1)} %bitcast.13) | data formatting | bytes 2097152
Async XLA Ops:
  0.6 1.2 %copy-start = (bf16[512,4,2,128]{3,2,1,0:T(2,128)(2,1)S(1)}, bf16[512,4,2,128]{3,2,1,0:T(2,128)(2,1)}, u32[]{:S(2)}) copy-start(bf16[512,4,2,128]{3,2,1,0:T(2,128)(2,1)} %param.6) | copy-start | bytes 3145732
  1.9 1.2 %copy-start.1 = (bf16[512,4,2,128]{3,2,1,0:T(2,128)(2,1)S(1)}, bf16[512,4,2,128]{3,2,1,0:T(2,128)(2,1)}, u32[]{:S(2)}) copy-start(bf16[512,4,2,128]{3,2,1,0:T(2,128)(2,1)} %param.9) | copy-start | bytes 3145732
  3.1 1.0 %copy-start.2 = (bf16[512,4,128]{2,1,0:T(4,128)(2,1)S(1)}, bf16[512,4,128]{2,1,0:T(4,128)(2,1)}, u32[]{:S(2)}) copy-start(bf16[512,4,128]{2,1,0:T(4,128)(2,1)} %param.7) | copy-start | bytes 1572868
  4.1 1.0 %copy-start.3 = (bf16[512,4,128]{2,1,0:T(4,128)(2,1)S(1)}, bf16[512,4,128]{2,1,0:T(4,128)(2,1)}, u32[]{:S(2)}) copy-start(bf16[512,4,128]{2,1,0:T(4,128)(2,1)} %param.8) | copy-start | bytes 1572868
  5.2 0.7 copy-start.4
  5.8 0.7 copy-start.5
